TPU v7x, 32 devices: a whole 2x2x4 slice. The times are simulated.
32 devices in a mesh: xy: 8 (over y, x, core), gz: 4 (over z).
Axes of the slice: x: 2, y: 2, z: 4, core: 2. Of those that a mesh axis runs over, the one named last changes fastest.
Arguments:
- velocity: float32 [3, 16, 256, 1024], P(None, 'gz', 'xy'), may hold values from -6 to 6
- magnetic: float32 [3, 8, 128, 512], P(None, 'gz', 'xy'), may hold values from -6 to 6
- slot_block_table: int32 [256], P('xy'), may hold values from 0 to 255, as said below
Outputs:
- updated_fine_velocity: float32 [3, 16, 256, 1024], P(None, 'gz', 'xy')
- magnetic_next: float32 [3, 8, 128, 512], P(None, 'gz', 'xy')
Inputs may be any that keep to these rules, and one draw needn't show every extreme that they name: `slot_block_table`: each block number appears in one slot; the 32 slots of one device along xy hold exactly 4 blocks of every block row.
All inputs are finite; a program needn't handle non-finite values.
Results may differ from a plain program's by a relative error of at most 0.00005.
Values sent between devices are 32-bit elements; how exact they have to be, the bound alone decides.
No kernel may reach another device: no remote copies, remote signals or barrier semaphores. Data moves between devices by JAX's collectives and lax.ppermute only.
A program may use at most 64 MiB of HBM per device.

v0:
```python
import jax
import jax.numpy as jnp
from jax import lax
from jax.sharding import PartitionSpec as P

BLOCK_EDGE = 32


def with_halo(value, sides, width):
    for axis, dim in sides:
        size, length = (lax.axis_size(axis), value.shape[dim])
        up = [(i, (i + 1) % size) for i in range(size)]
        down = [(j, i) for i, j in up]
        last = lax.slice_in_dim(value, length - width, length, axis=dim)
        first = lax.slice_in_dim(value, 0, width, axis=dim)
        before = lax.ppermute(last, axis, up)
        after = lax.ppermute(first, axis, down)
        value = jnp.concatenate([before, value, after], axis=dim)
    return value


def restrict(fine, blk):
    half_width = blk // 2
    s = fine.shape
    v = fine.reshape(s[0], s[1] // 2, 2, s[2], half_width, 2, half_width, 2)
    return (jnp.sum(v, axis=(2, 5, 7)) * 0.125).reshape(
        s[0], s[1] // 2, s[2], half_width * half_width
    )


def inner(padded):
    return padded[:, 1:-1, 1:-1]


def along_z(padded):
    return (padded[:, 2:, 1:-1] - padded[:, :-2, 1:-1]) * 0.5


def along_y(padded):
    return (padded[:, 1:-1, 2:] - padded[:, 1:-1, :-2]) * 0.5


def along_x(padded):
    middle = inner(padded)
    return (jnp.roll(middle, -1, 3) - jnp.roll(middle, 1, 3)) * 0.5


def curl_padded(padded):
    dzv = along_z(padded)
    dyv = along_y(padded)
    dxv = along_x(padded)
    return jnp.stack([dyv[2] - dzv[1], dzv[0] - dxv[2], dxv[1] - dyv[0]])


def cross(a, b):
    return jnp.stack(
        [a[1] * b[2] - a[2] * b[1], a[2] * b[0] - a[0] * b[2], a[0] * b[1] - a[1] * b[0]]
    )


def laplace_padded(padded):
    middle = inner(padded)
    total = padded[:, 2:, 1:-1] + padded[:, :-2, 1:-1] + padded[:, 1:-1, 2:] + padded[:, 1:-1, :-2]
    return total + jnp.roll(middle, 1, 3) + jnp.roll(middle, -1, 3) - 6.0 * middle


def split_into_tiles(magnetic_state, coarse_depth_index, half_width, slot_count):
    return (
        magnetic_state.reshape(
            magnetic_state.shape[0], coarse_depth_index, half_width, slot_count, half_width
        )
        .transpose(0, 1, 3, 2, 4)
        .reshape(magnetic_state.shape[0], coarse_depth_index, slot_count, half_width * half_width)
    )


def assemble_from_tiles(tile_stack, coarse_depth_index, half_width, slot_count):
    return (
        tile_stack.reshape(
            tile_stack.shape[0], coarse_depth_index, slot_count, half_width, half_width
        )
        .transpose(0, 1, 3, 2, 4)
        .reshape(tile_stack.shape[0], coarse_depth_index, half_width, slot_count * half_width)
    )


def body(velocity, magnetic, slot_block_table):
    half_width = BLOCK_EDGE // 2
    slot_count = velocity.shape[2]
    coarse_depth_index = velocity.shape[1] // 2
    column_indices = slot_block_table % slot_count
    sorted_positions = jnp.argsort(slot_block_table)
    dispatched_columns = column_indices[sorted_positions].reshape(1, 1, slot_count, 1)
    ordered = velocity[:, :, sorted_positions]
    got, received_columns = (
        lax.all_to_all(
            restrict(ordered, BLOCK_EDGE), "xy", split_axis=2, concat_axis=2, tiled=True
        ),
        lax.all_to_all(dispatched_columns, "xy", split_axis=2, concat_axis=2, tiled=True),
    )
    column_listing = received_columns.reshape(slot_count)
    grouped_by_column = got[:, :, jnp.argsort(column_listing)]
    coarse_flow_field = assemble_from_tiles(
        grouped_by_column, coarse_depth_index, half_width, slot_count
    )
    emf = cross(coarse_flow_field, magnetic)
    stacked = jnp.concatenate([magnetic, emf], axis=0)
    padded = with_halo(stacked, (("xy", 2), ("gz", 1)), 1)
    field_pad = padded[0:3]
    current = curl_padded(field_pad)
    magnetic_next = magnetic + 0.1 * (curl_padded(padded[3:6]) + 0.5 * laplace_padded(field_pad))
    lorentz_force = cross(current, magnetic)
    returned_back_tiles = split_into_tiles(
        lorentz_force, coarse_depth_index, half_width, slot_count
    )[:, :, column_listing]
    returned = lax.all_to_all(returned_back_tiles, "xy", split_axis=2, concat_axis=2, tiled=True)
    blocks_per_slot = returned[:, :, jnp.argsort(sorted_positions)]
    widened_tiles = jnp.broadcast_to(
        blocks_per_slot.reshape(3, coarse_depth_index, 1, slot_count, half_width, 1, half_width, 1),
        (3, coarse_depth_index, 2, slot_count, half_width, 2, half_width, 2),
    )
    updated_fine_velocity = velocity + 0.1 * widened_tiles.reshape(
        3, coarse_depth_index * 2, slot_count, BLOCK_EDGE * BLOCK_EDGE
    )
    return (updated_fine_velocity, magnetic_next)


def solution(mesh):
    return jax.shard_map(
        body,
        mesh=mesh,
        in_specs=(P(None, "gz", "xy", None), P(None, "gz", "xy", None), P("xy")),
        out_specs=(P(None, "gz", "xy", None), P(None, "gz", "xy", None)),
        check_vma=False,
    )
```

profile of v0, /device:TPU:0, one launch (start us, length us, event | category | flops | bytes accessed | tf_op | source)
XLA Modules:
  0.0 104.9 jit_solution(8437130082161293835)
XLA Ops:
  0.6 0.8 and_select_fusion
  1.4 2.3 %sort.45 = (s32[32]{0:T(128)}, s32[32]{0:T(128)S(1)}) sort(s32[32]{0:T(128)} %param.5, s32[32]{0:T(128)S(1)} %iota.10), dimensions={0}, to_apply=%region_0.1 | sort | flops 160 | bytes 512 | tf_op jit(solution)/shard_map/jit(argsort)/sort | solution.py:92
  3.7 0.6 copy-done.19
  4.3 0.7 gather_fusion.1
  5.0 0.7 copy.33
  5.7 5.2 %all-to-all-start.1 = ((s32[1,1,32,1]{3,1,0,2:T(1,128)}), s32[1,1,32,1]{3,1,0,2:T(1,128)S(1)}, u32[]{:S(2)}, u32[]{:S(2)}) async-start(s32[1,1,32,1]{3,1,0,2:T(1,128)} %copy.33), calls=%async_computation.1 | async-start | bytes 32768 | tf_op jit(solution)/shard_map/all_to_all | solution.py:99
  10.9 1.5 %fusion.14 = (f32[3,2,16,1]{3,2,1,0:T(8,128)}, f32[3,2,16,1]{3,2,1,0:T(8,128)}) fusion(f32[3,2,16,512]{3,2,1,0:T(8,128)} %param.4), kind=kLoop, calls=%fused_computation.82 | loop fusion | bytes 1536 | tf_op jit(solution)/shard_map/jit(_roll_static)/slice | solution.py:45
  12.4 1.1 %fusion.13 = (f32[3,2,16,511]{3,2,1,0:T(8,128)S(1)}, f32[3,2,16,511]{3,2,1,0:T(8,128)S(1)}) fusion(f32[3,2,16,512]{3,2,1,0:T(8,128)} %param.4), kind=kLoop, calls=%fused_computation.81 | loop fusion | bytes 784896 | tf_op jit(solution)/shard_map/jit(_roll_static)/slice | solution.py:45
  13.6 3.0 %gather_fusion = f32[32,3,4,1024]{3,0,2,1:T(8,128)S(1)} fusion(f32[3,4,32,1024]{3,2,1,0:T(8,128)S(1)} %copy-done, s32[1024]{0:T(1024)} %copy-done.18), kind=kCustom, calls=%fused_computation | custom fusion | bytes 3145856 | tf_op jit(solution)/shard_map/gather | solution.py:94
  16.5 4.0 %copy.43 = f32[3,4,32,1024]{2,3,1,0:T(8,128)} copy(f32[3,4,32,1024]{3,2,1,0:T(8,128)S(1)} %copy-done) | data formatting | bytes 3145728 | tf_op args[0]
  20.5 2.3 %sort.47 = (s32[32]{0:T(128)}, s32[32]{0:T(128)S(1)}) sort(s32[32]{0:T(128)} %copy-done.19, s32[32]{0:T(128)S(1)} %iota.12), dimensions={0}, to_apply=%region_3.4 | sort | flops 160 | bytes 512 | tf_op jit(solution)/shard_map/jit(argsort)/sort | solution.py:117
  22.8 0.6 pad_clamp_fusion
  23.4 4.0 %copy.31 = f32[3,4,32,1024]{2,3,1,0:T(8,128)} copy(f32[3,4,32,1024]{3,2,1,0:T(8,128)S(1)} %bitcast.34) | data formatting | bytes 3145728 | tf_op jit(solution)/shard_map/gather | solution.py:94
  27.3 7.3 %reduce_sum.9 = f32[3,2,32,16,16]{2,4,3,1,0:T(8,128)S(1)} reduce(f32[3,2,2,32,16,2,16,2]{3,7,6,5,4,2,1,0:T(2,128)} %bitcast.32, f32[]{:T(128)} %constant.10.clone.1), dimensions={2,5,7}, to_apply=%region_1.2 | reduce | flops 344064 | bytes 1769476 | tf_op jit(solution)/shard_map/reduce_sum | solution.py:26
  34.7 0.7 copy-done.12
  35.6 0.9 copy.32
  36.5 4.2 %all-to-all-start = ((f32[3,2,32,256]{3,1,0,2:T(2,128)}), f32[3,2,32,256]{3,1,0,2:T(2,128)S(1)}, u32[]{:S(2)}, u32[]{:S(2)}) async-start(f32[3,2,32,256]{3,1,0,2:T(2,128)} %copy.32), calls=%async_computation | async-start | bytes 393216 | tf_op jit(solution)/shard_map/all_to_all | solution.py:96
  40.7 0.7 reduce
  41.4 1.6 %sort.46 = (s32[32]{0:T(128)}, s32[32]{0:T(128)S(1)}) sort(s32[32]{0:T(128)S(1)} %reduce, s32[32]{0:T(128)S(1)} %iota.11), dimensions={0}, to_apply=%region_2.3 | sort | flops 160 | bytes 512 | tf_op jit(solution)/shard_map/jit(argsort)/sort | solution.py:102
  43.0 3.9 %all-to-all-done = f32[3,2,32,256]{3,1,0,2:T(2,128)S(1)} async-done(((f32[3,2,32,256]{3,1,0,2:T(2,128)}), f32[3,2,32,256]{3,1,0,2:T(2,128)S(1)}, u32[]{:S(2)}, u32[]{:S(2)}) %all-to-all-start) | async-done | bytes 196640 | tf_op jit(solution)/shard_map/all_to_all | solution.py:96
  46.9 0.8 gather_fusion.2
  47.7 0.3 copy.35
  48.3 0.3 squeeze.7
  48.8 0.3 squeeze.8
  49.3 0.3 squeeze.6
  49.8 2.6 %collective-permute-start.1 = (f32[6,2,1,512]{3,2,1,0:T(1,128)S(1)}, f32[6,2,1,512]{3,2,1,0:T(1,128)S(1)}, u32[]{:S(2)}, u32[]{:S(2)}) collective-permute-start(f32[6,2,1,512]{3,2,1,0:T(1,128)S(1)} %get-tuple-element.23), channel_id=1, source_target_pairs={{4,0},{8,4},{12,8},{16,12},{20,16},{24,20},{28,24},{0,28},{5,1},{9... | collective-permute-start | bytes 73736 | tf_op jit(solution)/shard_map/ppermute | solution.py:17
  52.4 1.7 %collective-permute-done = f32[6,2,1,512]{3,2,1,0:T(1,128)S(1)} collective-permute-done((f32[6,2,1,512]{3,2,1,0:T(1,128)S(1)}, f32[6,2,1,512]{3,2,1,0:T(1,128)S(1)}, u32[]{:S(2)}, u32[]{:S(2)}) %collective-permute-start) | collective-permute-done | bytes 24608 | tf_op jit(solution)/shard_map/ppermute | solution.py:16
  54.3 1.6 %collective-permute-start.3 = (f32[6,1,18,512]{3,2,1,0:T(8,128)S(1)}, f32[6,1,18,512]{3,2,1,0:T(8,128)S(1)}, u32[]{:S(2)}, u32[]{:S(2)}) collective-permute-start(f32[6,1,18,512]{3,2,1,0:T(8,128)S(1)} %get-tuple-element.20), channel_id=1, source_target_pairs={{0,1},{1,2},{2,3},{3,0},{4,5},{5,6},{6,7},{7,4},{8,9},{9,10},{10,1... | collective-permute-start | bytes 663560 | tf_op jit(solution)/shard_map/ppermute | solution.py:16
  55.9 2.3 %collective-permute-start.2 = (f32[6,1,18,512]{3,2,1,0:T(8,128)S(1)}, f32[6,1,18,512]{3,2,1,0:T(8,128)S(1)}, u32[]{:S(2)}, u32[]{:S(2)}) collective-permute-start(f32[6,1,18,512]{3,2,1,0:T(8,128)S(1)} %get-tuple-element.21), channel_id=1, source_target_pairs={{1,0},{2,1},{3,2},{0,3},{5,4},{6,5},{7,6},{4,7},{9,8},{10,9},{11,1... | collective-permute-start | bytes 663560 | tf_op jit(solution)/shard_map/ppermute | solution.py:17
  58.2 0.7 fusion.3
  59.0 7.1 %collective-permute-done.3 = f32[6,1,18,512]{3,2,1,0:T(8,128)S(1)} collective-permute-done((f32[6,1,18,512]{3,2,1,0:T(8,128)S(1)}, f32[6,1,18,512]{3,2,1,0:T(8,128)S(1)}, u32[]{:S(2)}, u32[]{:S(2)}) %collective-permute-start.3) | collective-permute-done | bytes 221216 | tf_op jit(solution)/shard_map/ppermute | solution.py:16
  66.0 4.7 %collective-permute-done.2 = f32[6,1,18,512]{3,2,1,0:T(8,128)S(1)} collective-permute-done((f32[6,1,18,512]{3,2,1,0:T(8,128)S(1)}, f32[6,1,18,512]{3,2,1,0:T(8,128)S(1)}, u32[]{:S(2)}, u32[]{:S(2)}) %collective-permute-start.2) | collective-permute-done | bytes 221216 | tf_op jit(solution)/shard_map/ppermute | solution.py:17
  70.7 0.7 fusion.1
  71.4 0.7 fusion.11
  72.1 0.8 fusion.12
  73.3 1.0 stack.23
  74.3 1.0 stack.22
  75.3 1.4 %maximum_bitcast_fusion = f32[3,2,32,16,16]{4,2,3,1,0:T(8,128)S(1)} fusion(f32[1,2,16,32,16]{4,3,2,1,0:T(8,128)} %stack.23, f32[1,2,16,32,16]{4,3,2,1,0:T(8,128)} %stack.22, f32[1,2,16,32,16]{4,3,2,1,0:T(8,128)S(1)} %stack.10), kind=kLoop, calls=%fused_computation.5 | loop fusion | flops 98304 | bytes 393216 | tf_op jit(solution)/shard_map/transpose | solution.py:72
  76.7 0.5 copy.39
  77.5 1.5 %gather_fusion.3 = f32[32,3,2,256]{3,2,1,0:T(2,128)} fusion(f32[3,2,32,256]{3,1,2,0:T(2,128)S(1)} %copy.40, s32[1024]{0:T(1024)S(1)} %pad_clamp_fusion.1), kind=kCustom, calls=%fused_computation.3 | custom fusion | bytes 393344 | tf_op jit(solution)/shard_map/gather | solution.py:113
  78.9 3.4 %all-to-all-start.2 = ((f32[3,2,32,256]{3,1,0,2:T(2,128)}), f32[3,2,32,256]{3,1,0,2:T(2,128)S(1)}, u32[]{:S(2)}, u32[]{:S(2)}) async-start(f32[3,2,32,256]{3,1,0,2:T(2,128)} %bitcast.11), calls=%async_computation.2 | async-start | bytes 393216 | tf_op jit(solution)/shard_map/all_to_all | solution.py:116
  82.6 0.9 fusion.6
  83.5 5.0 %all-to-all-done.2 = f32[3,2,32,256]{3,1,0,2:T(2,128)S(1)} async-done(((f32[3,2,32,256]{3,1,0,2:T(2,128)}), f32[3,2,32,256]{3,1,0,2:T(2,128)S(1)}, u32[]{:S(2)}, u32[]{:S(2)}) %all-to-all-start.2) | async-done | bytes 196640 | tf_op jit(solution)/shard_map/all_to_all | solution.py:116
  88.5 0.9 gather_fusion.4
  89.5 0.3 copy.42
  89.8 3.2 %broadcast_in_dim.19 = f32[3,2,2,32,16,2,16,2]{3,7,6,5,4,2,1,0:T(2,128)S(1)} broadcast(f32[3,2,32,16,16]{2,4,3,1,0:T(8,128)S(1)} %bitcast.35), dimensions={0,1,3,4,6} | broadcast | bytes 1769472 | tf_op jit(solution)/shard_map/broadcast_in_dim | solution.py:118
  93.0 6.3 %add.55 = f32[3,4,32,1024]{2,3,1,0:T(8,128)} add(f32[3,4,32,1024]{2,3,1,0:T(8,128)} %copy.43, f32[3,4,32,1024]{2,3,1,0:T(8,128)S(1)} %bitcast.33) | non-fusion elementwise | flops 393216 | bytes 4718592 | tf_op jit(solution)/shard_map/add | solution.py:122
  99.3 5.5 %copy.44 = f32[3,4,32,1024]{3,2,1,0:T(8,128)} copy(f32[3,4,32,1024]{2,3,1,0:T(8,128)} %add.55) | data formatting | bytes 3145728
  (71 shorter events, 2.3 us)
Async XLA Ops:
  0.6 12.9 %copy-start = (f32[3,4,32,1024]{3,2,1,0:T(8,128)S(1)}, f32[3,4,32,1024]{3,2,1,0:T(8,128)}, u32[]{:S(2)}) copy-start(f32[3,4,32,1024]{3,2,1,0:T(8,128)} %param.3) | copy-start | bytes 4718596
  3.7 0.6 copy-start.19
  4.3 8.1 %copy-start.18 = (s32[1024]{0:T(1024)}, s32[1024]{0:T(1024)S(1)}, u32[]{:S(2)}) copy-start(s32[1024]{0:T(1024)S(1)} %pad_clamp_fusion.3) | copy-start | bytes 12292
  5.7 30.8 %all-to-all-start.1 = ((s32[1,1,32,1]{3,1,0,2:T(1,128)}), s32[1,1,32,1]{3,1,0,2:T(1,128)S(1)}, u32[]{:S(2)}, u32[]{:S(2)}) async-start(s32[1,1,32,1]{3,1,0,2:T(1,128)} %copy.33), calls=%async_computation.1 | async-start | bytes 32768 | tf_op jit(solution)/shard_map/all_to_all | solution.py:99
  13.6 21.2 %copy-start.2 = (f32[3,2,16,511]{3,2,1,0:T(8,128)}, f32[3,2,16,511]{3,2,1,0:T(8,128)S(1)}, u32[]{:S(2)}) copy-start(f32[3,2,16,511]{3,2,1,0:T(8,128)S(1)} %get-tuple-element.37) | copy-start | bytes 588676
  34.6 0.8 copy-start.12
  34.6 0.8 copy-start.14
  36.5 10.4 %all-to-all-start = ((f32[3,2,32,256]{3,1,0,2:T(2,128)}), f32[3,2,32,256]{3,1,0,2:T(2,128)S(1)}, u32[]{:S(2)}, u32[]{:S(2)}) async-start(f32[3,2,32,256]{3,1,0,2:T(2,128)} %copy.32), calls=%async_computation | async-start | bytes 393216 | tf_op jit(solution)/shard_map/all_to_all | solution.py:96
  48.3 1.3 %copy-start.1 = (f32[3,2,16,512]{3,2,1,0:T(8,128)S(1)}, f32[3,2,16,512]{3,2,1,0:T(8,128)}, u32[]{:S(2)}) copy-start(f32[3,2,16,512]{3,2,1,0:T(8,128)} %param.4) | copy-start | bytes 589828
  49.7 4.4 %collective-permute-start = (f32[6,2,1,512]{3,2,1,0:T(1,128)S(1)}, f32[6,2,1,512]{3,2,1,0:T(1,128)S(1)}, u32[]{:S(2)}, u32[]{:S(2)}) collective-permute-start(f32[6,2,1,512]{3,2,1,0:T(1,128)S(1)} %get-tuple-element.22), channel_id=1, source_target_pairs={{0,4},{4,8},{8,12},{12,16},{16,20},{20,24},{24,28},{28,0},{1,5},{5... | collective-permute-start | bytes 73736 | tf_op jit(solution)/shard_map/ppermute | solution.py:16
  49.8 4.4 %collective-permute-start.1 = (f32[6,2,1,512]{3,2,1,0:T(1,128)S(1)}, f32[6,2,1,512]{3,2,1,0:T(1,128)S(1)}, u32[]{:S(2)}, u32[]{:S(2)}) collective-permute-start(f32[6,2,1,512]{3,2,1,0:T(1,128)S(1)} %get-tuple-element.23), channel_id=1, source_target_pairs={{4,0},{8,4},{12,8},{16,12},{20,16},{24,20},{28,24},{0,28},{5,1},{9... | collective-permute-start | bytes 73736 | tf_op jit(solution)/shard_map/ppermute | solution.py:17
  54.1 18.8 %copy-start.4 = (f32[6,2,1,512]{3,2,1,0:T(1,128)}, f32[6,2,1,512]{3,2,1,0:T(1,128)S(1)}, u32[]{:S(2)}) copy-start(f32[6,2,1,512]{3,2,1,0:T(1,128)S(1)} %collective-permute-done) | copy-start | bytes 73732
  54.1 18.8 %copy-start.6 = (f32[6,2,1,512]{3,2,1,0:T(1,128)}, f32[6,2,1,512]{3,2,1,0:T(1,128)S(1)}, u32[]{:S(2)}) copy-start(f32[6,2,1,512]{3,2,1,0:T(1,128)S(1)} %collective-permute-done.1) | copy-start | bytes 73732
  54.3 11.8 %collective-permute-start.3 = (f32[6,1,18,512]{3,2,1,0:T(8,128)S(1)}, f32[6,1,18,512]{3,2,1,0:T(8,128)S(1)}, u32[]{:S(2)}, u32[]{:S(2)}) collective-permute-start(f32[6,1,18,512]{3,2,1,0:T(8,128)S(1)} %get-tuple-element.20), channel_id=1, source_target_pairs={{0,1},{1,2},{2,3},{3,0},{4,5},{5,6},{6,7},{7,4},{8,9},{9,10},{10,1... | collective-permute-start | bytes 663560 | tf_op jit(solution)/shard_map/ppermute | solution.py:16
  55.9 14.8 %collective-permute-start.2 = (f32[6,1,18,512]{3,2,1,0:T(8,128)S(1)}, f32[6,1,18,512]{3,2,1,0:T(8,128)S(1)}, u32[]{:S(2)}, u32[]{:S(2)}) collective-permute-start(f32[6,1,18,512]{3,2,1,0:T(8,128)S(1)} %get-tuple-element.21), channel_id=1, source_target_pairs={{1,0},{2,1},{3,2},{0,3},{5,4},{6,5},{7,6},{4,7},{9,8},{10,9},{11,1... | collective-permute-start | bytes 663560 | tf_op jit(solution)/shard_map/ppermute | solution.py:17
  77.1 5.2 %copy-start.8 = (f32[3,2,16,511]{3,2,1,0:T(8,128)S(1)}, f32[3,2,16,511]{3,2,1,0:T(8,128)}, u32[]{:S(2)}) copy-start(f32[3,2,16,511]{3,2,1,0:T(8,128)} %get-tuple-element.34) | copy-start | bytes 588676
  77.1 5.2 %copy-start.9 = (f32[3,2,16,511]{3,2,1,0:T(8,128)S(1)}, f32[3,2,16,511]{3,2,1,0:T(8,128)}, u32[]{:S(2)}) copy-start(f32[3,2,16,511]{3,2,1,0:T(8,128)} %get-tuple-element.35) | copy-start | bytes 588676
  77.1 5.2 %copy-start.16 = (f32[3,2,16,1]{3,2,1,0:T(8,128)S(1)}, f32[3,2,16,1]{3,2,1,0:T(8,128)}, u32[]{:S(2)}) copy-start(f32[3,2,16,1]{3,2,1,0:T(8,128)} %get-tuple-element.32) | copy-start | bytes 1156
  77.1 5.2 %copy-start.17 = (f32[3,2,16,1]{3,2,1,0:T(8,128)S(1)}, f32[3,2,16,1]{3,2,1,0:T(8,128)}, u32[]{:S(2)}) copy-start(f32[3,2,16,1]{3,2,1,0:T(8,128)} %get-tuple-element.33) | copy-start | bytes 1156
  77.2 5.4 %copy-start.10 = (f32[3,2,16,512]{3,2,1,0:T(8,128)S(1)}, f32[3,2,16,512]{3,2,1,0:T(8,128)}, u32[]{:S(2)}) copy-start(f32[3,2,16,512]{3,2,1,0:T(8,128)} %fusion.3) | copy-start | bytes 589828
  77.2 5.4 %copy-start.11 = (f32[3,2,16,512]{3,2,1,0:T(8,128)S(1)}, f32[3,2,16,512]{3,2,1,0:T(8,128)}, u32[]{:S(2)}) copy-start(f32[3,2,16,512]{3,2,1,0:T(8,128)} %get-tuple-element.30) | copy-start | bytes 589828
  77.2 5.4 %copy-start.3 = (f32[3,2,16,511]{3,2,1,0:T(8,128)S(1)}, f32[3,2,16,511]{3,2,1,0:T(8,128)}, u32[]{:S(2)}) copy-start(f32[3,2,16,511]{3,2,1,0:T(8,128)} %copy-done.2) | copy-start | bytes 588676
  77.2 5.4 %copy-start.5 = (f32[6,2,1,512]{3,2,1,0:T(1,128)S(1)}, f32[6,2,1,512]{3,2,1,0:T(1,128)}, u32[]{:S(2)}) copy-start(f32[6,2,1,512]{3,2,1,0:T(1,128)} %copy-done.4) | copy-start | bytes 73732
  77.2 5.4 %copy-start.7 = (f32[6,2,1,512]{3,2,1,0:T(1,128)S(1)}, f32[6,2,1,512]{3,2,1,0:T(1,128)}, u32[]{:S(2)}) copy-start(f32[6,2,1,512]{3,2,1,0:T(1,128)} %copy-done.6) | copy-start | bytes 73732
  77.2 5.4 %copy-start.13 = (f32[3,2,16,1]{3,2,1,0:T(8,128)S(1)}, f32[3,2,16,1]{3,2,1,0:T(8,128)}, u32[]{:S(2)}) copy-start(f32[3,2,16,1]{3,2,1,0:T(8,128)} %get-tuple-element.38) | copy-start | bytes 1156
  77.2 5.4 %copy-start.15 = (f32[3,2,16,1]{3,2,1,0:T(8,128)S(1)}, f32[3,2,16,1]{3,2,1,0:T(8,128)}, u32[]{:S(2)}) copy-start(f32[3,2,16,1]{3,2,1,0:T(8,128)} %get-tuple-element.39) | copy-start | bytes 1156
  78.9 9.5 %all-to-all-start.2 = ((f32[3,2,32,256]{3,1,0,2:T(2,128)}), f32[3,2,32,256]{3,1,0,2:T(2,128)S(1)}, u32[]{:S(2)}, u32[]{:S(2)}) async-start(f32[3,2,32,256]{3,1,0,2:T(2,128)} %bitcast.11), calls=%async_computation.2 | async-start | bytes 393216 | tf_op jit(solution)/shard_map/all_to_all | solution.py:116
where the time goes:
time: 106 us; the launch traced here: 105 us
  local copies, waits for them, and re-layouts  35.8 us (34%)
  other arithmetic  26.2 us (25%)
  waiting for transfers between devices  22.3 us (21%)
  starting transfers between devices  19.4 us (18%)
  between operations  1.12 us (1%)
    unnamed x42, local copies, waits for them, and re-layouts  10.9 us
    ppermute x2, waiting for transfers between devices, with_halo(): before = lax.ppermute(last, axis, up)  8.8 us
    reduce_sum x1, other arithmetic, restrict(): jnp.sum(v, axis=(2, 5, 7)) * 0.125  7.27 us
    gather x2, local copies, waits for them, and re-layouts, body(): ordered = velocity[:, :, sorted_positions]  6.93 us
    add x1, other arithmetic, body(): velocity + 0.1 * widened_tiles.reshape(3, coarse_depth_index * 2, slot_co...  6.28 us
    all_to_all x1, starting transfers between devices, body(): lax.all_to_all(dispatched_columns, 'xy', split_axis=2, concat_axis=2, til...  5.2 us
    all_to_all x1, waiting for transfers between devices, body(): lax.all_to_all(returned_back_tiles, 'xy', split_axis=2, concat_axis=2, ti...  4.99 us
    ppermute x2, starting transfers between devices, with_halo(): after = lax.ppermute(first, axis, down)  4.9 us
  transfers between devices with their start and end apart: 7, of which 5 were waited for; matrix products, arithmetic and copies ran while one was open for 28% of the time, Pallas kernels for 0%

commit v1 on v0

--- a/solution.py
+++ b/solution.py
@@ -93,8 +93,14 @@
     dispatched_columns = column_indices[sorted_positions].reshape(1, 1, slot_count, 1)
     ordered = velocity[:, :, sorted_positions]
     got, received_columns = (
-        lax.all_to_all(
-            restrict(ordered, BLOCK_EDGE), "xy", split_axis=2, concat_axis=2, tiled=True
+        jnp.concatenate(
+            lax.all_to_all(
+                jnp.stack(jnp.split(restrict(ordered, BLOCK_EDGE), lax.axis_size("xy"), axis=2)),
+                "xy",
+                0,
+                0,
+            ),
+            axis=2,
         ),
         lax.all_to_all(dispatched_columns, "xy", split_axis=2, concat_axis=2, tiled=True),
     )

time: 106 us -> 112 us (1.057)
  local copies, waits for them, and re-layouts: 35.8 us -> 43.7 us
  waiting for transfers between devices: 22.3 us -> 17 us
  other arithmetic: 26.2 us -> 29.9 us
    another operation x0 -> x2, local copies, waits for them, and re-layouts: none -> 5.41 us  [body(): jnp.stack(jnp.split(restrict(ordered, BLOCK_EDGE), lax.axis_size('xy'), a...]
    ppermute x2, waiting for transfers between devices: 8.8 us -> 4.3 us  [with_halo(): before = lax.ppermute(last, axis, up)]
    unnamed x42 -> x33, local copies, waits for them, and re-layouts: 10.9 us -> 14.4 us
    all_to_all x1, waiting for transfers between devices: 4.99 us -> 2.22 us  [body(): lax.all_to_all(returned_back_tiles, 'xy', split_axis=2, concat_axis=2, ti...]
    ppermute x2, waiting for transfers between devices: 4.65 us -> 6.58 us  [with_halo(): after = lax.ppermute(first, axis, down)]
    mul x2, other arithmetic: 0.26 us -> 1.99 us  [along_x(): return (jnp.roll(middle, -1, 3) - jnp.roll(middle, 1, 3)) * 0.5]
    ppermute x2, starting transfers between devices: 1.69 us -> 0.06 us  [with_halo(): before = lax.ppermute(last, axis, up)]
    ppermute x2, starting transfers between devices: 4.9 us -> 6.29 us  [with_halo(): after = lax.ppermute(first, axis, down)]
  transfers between devices with their start and end apart: 7 -> 7, of which waited for: 5 -> 4; matrix products, arithmetic and copies ran while one was open for 28% -> 35% of each run, Pallas kernels for 0% -> 0%
where the time goes in v1:
time: 112 us; the launch traced here: 111 us
  local copies, waits for them, and re-layouts  43.7 us (39%)
  other arithmetic  29.9 us (27%)
  starting transfers between devices  19.4 us (17%)
  waiting for transfers between devices  17 us (15%)
    unnamed x33, local copies, waits for them, and re-layouts  14.4 us
    reduce_sum x1, other arithmetic, restrict(): jnp.sum(v, axis=(2, 5, 7)) * 0.125  7.27 us
    gather x2, local copies, waits for them, and re-layouts, body(): ordered = velocity[:, :, sorted_positions]  6.92 us
    ppermute x2, waiting for transfers between devices, with_halo(): after = lax.ppermute(first, axis, down)  6.58 us
    ppermute x2, starting transfers between devices, with_halo(): after = lax.ppermute(first, axis, down)  6.29 us
    add x1, other arithmetic, body(): velocity + 0.1 * widened_tiles.reshape(3, coarse_depth_index * 2, slot_co...  6.28 us
    another operation x2, local copies, waits for them, and re-layouts, body(): jnp.stack(jnp.split(restrict(ordered, BLOCK_EDGE), lax.axis_size('xy'), a...  5.41 us
    all_to_all x1, starting transfers between devices, body(): lax.all_to_all(dispatched_columns, 'xy', split_axis=2, concat_axis=2, til...  5.2 us
  transfers between devices with their start and end apart: 7, of which 4 were waited for; matrix products, arithmetic and copies ran while one was open for 35% of the time, Pallas kernels for 0%

profile of v1, /device:TPU:0, one launch (start us, length us, event | category | flops | bytes accessed | tf_op | source)
XLA Modules:
  0.0 111.0 jit_solution(12348180995336600977)
XLA Ops:
  0.6 0.8 and_select_fusion
  1.4 2.3 %sort.45 = (s32[32]{0:T(128)}, s32[32]{0:T(128)S(1)}) sort(s32[32]{0:T(128)} %param.5, s32[32]{0:T(128)S(1)} %iota.10), dimensions={0}, to_apply=%region_0.1 | sort | flops 160 | bytes 512 | tf_op jit(solution)/shard_map/jit(argsort)/sort | solution.py:92
  3.7 0.5 copy-done.10
  4.2 0.7 gather_fusion.1
  4.9 0.7 copy.64
  5.6 5.2 %all-to-all-start.1 = ((s32[1,1,32,1]{3,1,0,2:T(1,128)}), s32[1,1,32,1]{3,1,0,2:T(1,128)S(1)}, u32[]{:S(2)}, u32[]{:S(2)}) async-start(s32[1,1,32,1]{3,1,0,2:T(1,128)} %copy.64), calls=%async_computation.1 | async-start | bytes 32768 | tf_op jit(solution)/shard_map/all_to_all | solution.py:105
  10.8 1.1 %fusion.21 = (f32[3,2,16,511]{3,2,1,0:T(8,128)S(1)}, f32[3,2,16,511]{3,2,1,0:T(8,128)S(1)}) fusion(f32[3,2,16,512]{3,2,1,0:T(8,128)} %param.4), kind=kLoop, calls=%fused_computation.97 | loop fusion | bytes 784896 | tf_op jit(solution)/shard_map/jit(_roll_static)/slice | solution.py:45
  12.0 1.6 %fusion.22 = (f32[3,2,16,1]{3,2,1,0:T(8,128)}, f32[3,2,16,1]{3,2,1,0:T(8,128)}) fusion(f32[3,2,16,512]{3,2,1,0:T(8,128)} %param.4), kind=kLoop, calls=%fused_computation.98 | loop fusion | bytes 1536 | tf_op jit(solution)/shard_map/jit(_roll_static)/slice | solution.py:45
  13.5 3.0 %gather_fusion = f32[32,3,4,1024]{3,0,2,1:T(8,128)S(1)} fusion(f32[3,4,32,1024]{3,2,1,0:T(8,128)S(1)} %copy-done, s32[1024]{0:T(1024)} %copy-done.9), kind=kCustom, calls=%fused_computation | custom fusion | bytes 3145856 | tf_op jit(solution)/shard_map/gather | solution.py:94
  16.5 4.0 %copy.61 = f32[3,4,32,1024]{2,3,1,0:T(8,128)} copy(f32[3,4,32,1024]{3,2,1,0:T(8,128)S(1)} %bitcast.76) | data formatting | bytes 3145728 | tf_op jit(solution)/shard_map/gather | solution.py:94
  20.5 7.3 %reduce_sum.9 = f32[3,2,32,16,16]{2,4,3,1,0:T(8,128)S(1)} reduce(f32[3,2,2,32,16,2,16,2]{3,7,6,5,4,2,1,0:T(2,128)} %bitcast.74, f32[]{:T(128)} %constant.10.clone.1), dimensions={2,5,7}, to_apply=%region_1.2 | reduce | flops 344064 | bytes 1769476 | tf_op jit(solution)/shard_map/reduce_sum | solution.py:26
  28.2 0.3 fusion.5
  28.4 0.3 fusion.4
  28.7 0.3 fusion.3
  29.8 2.6 %copy-done.2 = f32[8,3,2,4,256]{3,4,2,1,0:T(8,128)} copy-done((f32[8,3,2,4,256]{3,4,2,1,0:T(8,128)}, f32[8,3,2,4,256]{3,4,2,1,0:T(8,128)S(1)}, u32[]{:S(2)}) %copy-start.2) | copy-done | bytes 196632
  32.5 1.6 %sort.47 = (s32[32]{0:T(128)}, s32[32]{0:T(128)S(1)}) sort(s32[32]{0:T(128)S(1)} %copy-done.11, s32[32]{0:T(128)S(1)} %iota.12), dimensions={0}, to_apply=%region_3.4 | sort | flops 160 | bytes 512 | tf_op jit(solution)/shard_map/jit(argsort)/sort | solution.py:123
  34.1 0.6 compare_select_fusion
  34.7 0.8 subtract_multiply_fusion.1
  35.5 5.1 %copy.62 = f32[8,3,2,4,256]{4,3,2,1,0:T(4,128)} copy(f32[8,3,2,4,256]{3,4,2,1,0:T(8,128)} %copy-done.2) | data formatting | bytes 393216 | tf_op jit(solution)/shard_map/stack | solution.py:98
  40.6 4.2 %all-to-all-start = ((f32[8,3,2,4,256]{4,3,2,1,0:T(4,128)}), f32[8,3,2,4,256]{4,3,2,1,0:T(4,128)S(1)}, u32[]{:S(2)}, u32[]{:S(2)}) async-start(f32[8,3,2,4,256]{4,3,2,1,0:T(4,128)} %copy.62), calls=%async_computation | async-start | bytes 393216 | tf_op jit(solution)/shard_map/all_to_all | solution.py:97
  44.8 0.7 reduce
  45.5 1.6 %sort.46 = (s32[32]{0:T(128)}, s32[32]{0:T(128)S(1)}) sort(s32[32]{0:T(128)S(1)} %reduce, s32[32]{0:T(128)S(1)} %iota.11), dimensions={0}, to_apply=%region_2.3 | sort | flops 160 | bytes 512 | tf_op jit(solution)/shard_map/jit(argsort)/sort | solution.py:108
  47.1 3.9 %all-to-all-done = f32[8,3,2,4,256]{4,3,2,1,0:T(4,128)S(1)} async-done(((f32[8,3,2,4,256]{4,3,2,1,0:T(4,128)}), f32[8,3,2,4,256]{4,3,2,1,0:T(4,128)S(1)}, u32[]{:S(2)}, u32[]{:S(2)}) %all-to-all-start) | async-done | bytes 196640 | tf_op jit(solution)/shard_map/all_to_all | solution.py:97
  51.1 0.8 gather_fusion.2
  53.9 2.6 %collective-permute-start.1 = (f32[6,2,1,512]{3,2,1,0:T(1,128)S(1)}, f32[6,2,1,512]{3,2,1,0:T(1,128)S(1)}, u32[]{:S(2)}, u32[]{:S(2)}) collective-permute-start(f32[6,2,1,512]{3,2,1,0:T(1,128)S(1)} %get-tuple-element.25), channel_id=1, source_target_pairs={{4,0},{8,4},{12,8},{16,12},{20,16},{24,20},{28,24},{0,28},{5,1},{9... | collective-permute-start | bytes 73736 | tf_op jit(solution)/shard_map/ppermute | solution.py:17
  56.6 0.7 pad_clamp_fusion
  57.2 4.0 %copy.73 = f32[3,4,32,1024]{2,3,1,0:T(8,128)} copy(f32[3,4,32,1024]{3,2,1,0:T(8,128)S(1)} %copy-done) | data formatting | bytes 3145728 | tf_op args[0]
  61.4 3.7 %collective-permute-start.2 = (f32[6,1,18,512]{3,2,1,0:T(8,128)S(1)}, f32[6,1,18,512]{3,2,1,0:T(8,128)S(1)}, u32[]{:S(2)}, u32[]{:S(2)}) collective-permute-start(f32[6,1,18,512]{3,2,1,0:T(8,128)S(1)} %get-tuple-element.23), channel_id=1, source_target_pairs={{1,0},{2,1},{3,2},{0,3},{5,4},{6,5},{7,6},{4,7},{9,8},{10,9},{11,1... | collective-permute-start | bytes 663560 | tf_op jit(solution)/shard_map/ppermute | solution.py:17
  65.0 0.7 fusion.11
  65.8 6.6 %collective-permute-done.2 = f32[6,1,18,512]{3,2,1,0:T(8,128)S(1)} collective-permute-done((f32[6,1,18,512]{3,2,1,0:T(8,128)S(1)}, f32[6,1,18,512]{3,2,1,0:T(8,128)S(1)}, u32[]{:S(2)}, u32[]{:S(2)}) %collective-permute-start.2) | collective-permute-done | bytes 221216 | tf_op jit(solution)/shard_map/ppermute | solution.py:17
  72.4 4.3 %collective-permute-done.3 = f32[6,1,18,512]{3,2,1,0:T(8,128)S(1)} collective-permute-done((f32[6,1,18,512]{3,2,1,0:T(8,128)S(1)}, f32[6,1,18,512]{3,2,1,0:T(8,128)S(1)}, u32[]{:S(2)}, u32[]{:S(2)}) %collective-permute-start.3) | collective-permute-done | bytes 221216 | tf_op jit(solution)/shard_map/ppermute | solution.py:16
  76.7 0.7 fusion.9
  77.5 0.8 fusion.20
  78.3 0.7 fusion.19
  79.3 1.0 stack.58
  80.3 1.0 stack.59
  81.3 1.4 %maximum_bitcast_fusion = f32[3,2,32,16,16]{4,2,3,1,0:T(8,128)S(1)} fusion(f32[1,2,16,32,16]{4,3,2,1,0:T(8,128)} %stack.59, f32[1,2,16,32,16]{4,3,2,1,0:T(8,128)} %stack.58, f32[1,2,16,32,16]{4,3,2,1,0:T(8,128)S(1)} %stack.57), kind=kLoop, calls=%fused_computation.5 | loop fusion | flops 98304 | bytes 393216 | tf_op jit(solution)/shard_map/transpose | solution.py:72
  82.8 0.5 copy.69
  83.5 1.5 %gather_fusion.3 = f32[32,3,2,256]{3,2,1,0:T(2,128)} fusion(f32[3,2,32,256]{3,1,2,0:T(2,128)S(1)} %copy.70, s32[1024]{0:T(1024)S(1)} %get-tuple-element.42), kind=kCustom, calls=%fused_computation.3 | custom fusion | bytes 393344 | tf_op jit(solution)/shard_map/gather | solution.py:119
  84.9 3.6 %all-to-all-start.2 = ((f32[3,2,32,256]{3,1,0,2:T(2,128)}), f32[3,2,32,256]{3,1,0,2:T(2,128)S(1)}, u32[]{:S(2)}, u32[]{:S(2)}) async-start(f32[3,2,32,256]{3,1,0,2:T(2,128)} %bitcast.21), calls=%async_computation.2 | async-start | bytes 393216 | tf_op jit(solution)/shard_map/all_to_all | solution.py:122
  88.6 1.2 %fusion.12 = f32[3,2,16,512]{3,2,1,0:T(8,128)S(1)} fusion(f32[3,2,16,1]{3,2,1,0:T(8,128)} %get-tuple-element.35, f32[3,2,16,511]{3,2,1,0:T(8,128)} %get-tuple-element.37, f32[3,2,16,511]{3,2,1,0:T(8,128)} %get-tuple-element.36, f32[3,2,16,1]{3,2,1,0:T(8,128)} %get-tuple-element.34), kind=kLoop, calls=%fused_computation.56 | loop fusion | flops 196608 | bytes 589824 | tf_op jit(solution)/shard_map/mul | solution.py:45
  89.8 1.0 slice_subtract_fusion.2
  90.7 1.8 %fusion.14 = f32[3,2,16,512]{3,2,1,0:T(8,128)} fusion(f32[3,2,16,512]{3,2,1,0:T(8,128)S(1)} %copy-done.1, f32[1,2,16,512]{3,2,1,0:T(8,128)S(1)} %get-tuple-element.30, f32[1,2,16,512]{3,2,1,0:T(8,128)S(1)} %get-tuple-element.31, f32[1,2,16,512]{3,2,1,0:T(8,128)S(1)} %get-tuple-element.29, f32[3,2,16,511]{3,2,1,0:T(8,128)} %copy-done.3, ...), kind=kLoop, calls=%fused_computation.59 | loop fusion | flops 1720320 | bytes 1671168 | tf_op jit(solution)/shard_map/add | solution.py:117
  92.6 2.2 %all-to-all-done.2 = f32[3,2,32,256]{3,1,0,2:T(2,128)S(1)} async-done(((f32[3,2,32,256]{3,1,0,2:T(2,128)}), f32[3,2,32,256]{3,1,0,2:T(2,128)S(1)}, u32[]{:S(2)}, u32[]{:S(2)}) %all-to-all-start.2) | async-done | bytes 196640 | tf_op jit(solution)/shard_map/all_to_all | solution.py:122
  94.8 0.8 gather_fusion.4
  96.0 3.2 %broadcast_in_dim.19 = f32[3,2,2,32,16,2,16,2]{3,7,6,5,4,2,1,0:T(2,128)S(1)} broadcast(f32[3,2,32,16,16]{2,4,3,1,0:T(8,128)S(1)} %bitcast.77), dimensions={0,1,3,4,6} | broadcast | bytes 1769472 | tf_op jit(solution)/shard_map/broadcast_in_dim | solution.py:124
  99.2 6.3 %add.55 = f32[3,4,32,1024]{2,3,1,0:T(8,128)} add(f32[3,4,32,1024]{2,3,1,0:T(8,128)} %copy.73, f32[3,4,32,1024]{2,3,1,0:T(8,128)S(1)} %bitcast.75) | non-fusion elementwise | flops 393216 | bytes 4718592 | tf_op jit(solution)/shard_map/add | solution.py:128
  105.5 5.5 %copy.74 = f32[3,4,32,1024]{3,2,1,0:T(8,128)} copy(f32[3,4,32,1024]{2,3,1,0:T(8,128)} %add.55) | data formatting | bytes 3145728
  (62 shorter events, 4.5 us)
Async XLA Ops:
  0.6 12.9 %copy-start = (f32[3,4,32,1024]{3,2,1,0:T(8,128)S(1)}, f32[3,4,32,1024]{3,2,1,0:T(8,128)}, u32[]{:S(2)}) copy-start(f32[3,4,32,1024]{3,2,1,0:T(8,128)} %param.3) | copy-start | bytes 4718596
  3.7 0.5 copy-start.10
  4.2 1.4 %copy-start.9 = (s32[1024]{0:T(1024)}, s32[1024]{0:T(1024)S(1)}, u32[]{:S(2)}) copy-start(s32[1024]{0:T(1024)S(1)} %pad_clamp_fusion.3) | copy-start | bytes 12292
  5.6 35.0 %all-to-all-start.1 = ((s32[1,1,32,1]{3,1,0,2:T(1,128)}), s32[1,1,32,1]{3,1,0,2:T(1,128)S(1)}, u32[]{:S(2)}, u32[]{:S(2)}) async-start(s32[1,1,32,1]{3,1,0,2:T(1,128)} %copy.64), calls=%async_computation.1 | async-start | bytes 32768 | tf_op jit(solution)/shard_map/all_to_all | solution.py:105
  11.9 22.7 %copy-start.3 = (f32[3,2,16,511]{3,2,1,0:T(8,128)}, f32[3,2,16,511]{3,2,1,0:T(8,128)S(1)}, u32[]{:S(2)}) copy-start(f32[3,2,16,511]{3,2,1,0:T(8,128)S(1)} %get-tuple-element.39) | copy-start | bytes 588676
  27.8 4.7 %copy-start.11 = (s32[32]{0:T(128)S(1)}, s32[32]{0:T(128)}, u32[]{:S(2)}) copy-start(s32[32]{0:T(128)} %copy-done.10) | copy-start | bytes 388
  27.8 6.8 %copy-start.7 = (f32[3,2,16,1]{3,2,1,0:T(8,128)S(1)}, f32[3,2,16,1]{3,2,1,0:T(8,128)}, u32[]{:S(2)}) copy-start(f32[3,2,16,1]{3,2,1,0:T(8,128)} %get-tuple-element.40) | copy-start | bytes 1156
  27.8 6.8 %copy-start.8 = (f32[3,2,16,1]{3,2,1,0:T(8,128)S(1)}, f32[3,2,16,1]{3,2,1,0:T(8,128)}, u32[]{:S(2)}) copy-start(f32[3,2,16,1]{3,2,1,0:T(8,128)} %get-tuple-element.41) | copy-start | bytes 1156
  29.8 2.7 %copy-start.2 = (f32[8,3,2,4,256]{3,4,2,1,0:T(8,128)}, f32[8,3,2,4,256]{3,4,2,1,0:T(8,128)S(1)}, u32[]{:S(2)}) copy-start(f32[8,3,2,4,256]{3,4,2,1,0:T(8,128)S(1)} %fusion) | copy-start | bytes 589828
  35.5 18.3 %copy-start.1 = (f32[3,2,16,512]{3,2,1,0:T(8,128)S(1)}, f32[3,2,16,512]{3,2,1,0:T(8,128)}, u32[]{:S(2)}) copy-start(f32[3,2,16,512]{3,2,1,0:T(8,128)} %param.4) | copy-start | bytes 589828
  40.6 10.4 %all-to-all-start = ((f32[8,3,2,4,256]{4,3,2,1,0:T(4,128)}), f32[8,3,2,4,256]{4,3,2,1,0:T(4,128)S(1)}, u32[]{:S(2)}, u32[]{:S(2)}) async-start(f32[8,3,2,4,256]{4,3,2,1,0:T(4,128)} %copy.62), calls=%async_computation | async-start | bytes 393216 | tf_op jit(solution)/shard_map/all_to_all | solution.py:97
  53.9 7.3 %collective-permute-start = (f32[6,2,1,512]{3,2,1,0:T(1,128)S(1)}, f32[6,2,1,512]{3,2,1,0:T(1,128)S(1)}, u32[]{:S(2)}, u32[]{:S(2)}) collective-permute-start(f32[6,2,1,512]{3,2,1,0:T(1,128)S(1)} %get-tuple-element.24), channel_id=1, source_target_pairs={{0,4},{4,8},{8,12},{12,16},{16,20},{20,24},{24,28},{28,0},{1,5},{5... | collective-permute-start | bytes 73736 | tf_op jit(solution)/shard_map/ppermute | solution.py:16
  53.9 7.3 %collective-permute-start.1 = (f32[6,2,1,512]{3,2,1,0:T(1,128)S(1)}, f32[6,2,1,512]{3,2,1,0:T(1,128)S(1)}, u32[]{:S(2)}, u32[]{:S(2)}) collective-permute-start(f32[6,2,1,512]{3,2,1,0:T(1,128)S(1)} %get-tuple-element.25), channel_id=1, source_target_pairs={{4,0},{8,4},{12,8},{16,12},{20,16},{24,20},{28,24},{0,28},{5,1},{9... | collective-permute-start | bytes 73736 | tf_op jit(solution)/shard_map/ppermute | solution.py:17
  57.2 21.8 %copy-start.6 = (f32[3,2,16,512]{3,2,1,0:T(8,128)S(1)}, f32[3,2,16,512]{3,2,1,0:T(8,128)}, u32[]{:S(2)}) copy-start(f32[3,2,16,512]{3,2,1,0:T(8,128)} %subtract_multiply_fusion.1) | copy-start | bytes 589828
  61.2 17.9 %copy-start.4 = (f32[6,2,1,512]{3,2,1,0:T(1,128)}, f32[6,2,1,512]{3,2,1,0:T(1,128)S(1)}, u32[]{:S(2)}) copy-start(f32[6,2,1,512]{3,2,1,0:T(1,128)S(1)} %collective-permute-done) | copy-start | bytes 73732
  61.2 17.9 %copy-start.5 = (f32[6,2,1,512]{3,2,1,0:T(1,128)}, f32[6,2,1,512]{3,2,1,0:T(1,128)S(1)}, u32[]{:S(2)}) copy-start(f32[6,2,1,512]{3,2,1,0:T(1,128)S(1)} %collective-permute-done.1) | copy-start | bytes 73732
  61.4 11.1 %collective-permute-start.2 = (f32[6,1,18,512]{3,2,1,0:T(8,128)S(1)}, f32[6,1,18,512]{3,2,1,0:T(8,128)S(1)}, u32[]{:S(2)}, u32[]{:S(2)}) collective-permute-start(f32[6,1,18,512]{3,2,1,0:T(8,128)S(1)} %get-tuple-element.23), channel_id=1, source_target_pairs={{1,0},{2,1},{3,2},{0,3},{5,4},{6,5},{7,6},{4,7},{9,8},{10,9},{11,1... | collective-permute-start | bytes 663560 | tf_op jit(solution)/shard_map/ppermute | solution.py:17
  65.0 11.7 %collective-permute-start.3 = (f32[6,1,18,512]{3,2,1,0:T(8,128)S(1)}, f32[6,1,18,512]{3,2,1,0:T(8,128)S(1)}, u32[]{:S(2)}, u32[]{:S(2)}) collective-permute-start(f32[6,1,18,512]{3,2,1,0:T(8,128)S(1)} %get-tuple-element.22), channel_id=1, source_target_pairs={{0,1},{1,2},{2,3},{3,0},{4,5},{5,6},{6,7},{7,4},{8,9},{9,10},{10,1... | collective-permute-start | bytes 663560 | tf_op jit(solution)/shard_map/ppermute | solution.py:16
  84.9 9.8 %all-to-all-start.2 = ((f32[3,2,32,256]{3,1,0,2:T(2,128)}), f32[3,2,32,256]{3,1,0,2:T(2,128)S(1)}, u32[]{:S(2)}, u32[]{:S(2)}) async-start(f32[3,2,32,256]{3,1,0,2:T(2,128)} %bitcast.21), calls=%async_computation.2 | async-start | bytes 393216 | tf_op jit(solution)/shard_map/all_to_all | solution.py:122
